TPU v7x, 32 devices: a whole 2x2x4 slice. The times are simulated.
32 devices in a mesh: dp: 8 (over y, x, core), mp: 4 (over z).
Axes of the slice: x: 2, y: 2, z: 4, core: 2. Of those that a mesh axis runs over, the one named last changes fastest.
Arguments:
- act_in: bfloat16 [1024, 4096], P('dp', 'mp'), may hold values from -6 to 6
- grad_in: bfloat16 [1024, 16384], P('dp'), may hold values from -6 to 6
- query_act: bfloat16 [1024, 4096], P('dp', 'mp'), may hold values from -6 to 6
- query_grad: bfloat16 [1024, 16384], P('dp'), may hold values from -6 to 6
- act_basis: bfloat16 [4096, 128], P('mp'), may hold values from -1.1 to 1.1
- grad_basis: bfloat16 [16384, 128], P('dp'), may hold values from -1.1 to 1.1
- seq_lengths: int32 [4], replicated, may hold values from 1 to 256, 768 in all
Outputs:
- moments: float32 [4096, 16384], P('mp', 'dp')
- scores: float32 [64, 4], replicated
Inputs may be any that keep to these rules, and one draw needn't show every extreme that they name: `seq_lengths`: live tokens are the first ones of each sequence, and one sequence is full.
All inputs are finite; a program needn't handle non-finite values.
Results may differ from a plain program's by a relative error of at most 0.0046.
Values may be sent and summed in bfloat16 or wider, within the bound.
A program may use at most 192 MiB of HBM per device.

v0:
```python
import math
import jax
import jax.numpy as jnp
from jax import lax
from jax.sharding import PartitionSpec as P

D = 4096
FF = 16384
QUERIES = 64
QUERY_LEN = 16
damping = 0.1


def rotate(rows_in, basis_rows):
    count_rows, full_width = rows_in.shape
    block_size = basis_rows.shape[1]
    blocks = full_width // block_size
    product = jnp.einsum(
        "nbk,bkc->nbc",
        rows_in.reshape(count_rows, blocks, block_size),
        basis_rows.reshape(blocks, block_size, block_size),
        preferred_element_type=jnp.float32,
    )
    return product.reshape(count_rows, full_width)


def local(act_in, grad_in, query_act, query_grad, act_basis, grad_basis, seq_lengths):
    dp_count = lax.axis_size("dp")
    dp_index = lax.axis_index("dp")
    tok_dev = act_in.shape[0]
    seq_count = seq_lengths.shape[0]
    total_tokens = tok_dev * dp_count
    seq_len = total_tokens // seq_count
    global_rows = dp_index * tok_dev + jnp.arange(tok_dev, dtype=jnp.int32)
    seq_index = global_rows // seq_len
    within = global_rows % seq_len
    matches = seq_index[:, None] == jnp.arange(seq_count, dtype=jnp.int32)[None, :]
    row_length = jnp.sum(jnp.where(matches, seq_lengths[None, :], 0), axis=1)
    live_rows = (within < row_length).astype(jnp.float32)
    act_rot = (rotate(act_in, act_basis) * live_rows[:, None]).astype(jnp.bfloat16)
    query_act_rot = rotate(query_act, act_basis).astype(jnp.bfloat16)
    gathered_act, gathered_query = (
        lax.all_gather(act_rot, "dp", axis=0, tiled=True),
        lax.all_gather(query_act_rot, "dp", axis=0, tiled=True),
    )
    grad_cols, query_cols = (
        lax.all_to_all(grad_in, "dp", split_axis=1, concat_axis=0, tiled=True),
        lax.all_to_all(query_grad, "dp", split_axis=1, concat_axis=0, tiled=True),
    )
    grad_rot = rotate(grad_cols, grad_basis).astype(jnp.bfloat16)
    query_grad_rot = rotate(query_cols, grad_basis).astype(jnp.bfloat16)
    act_square = jnp.square(gathered_act.astype(jnp.float32)).astype(jnp.bfloat16)
    grad_square = jnp.square(grad_rot.astype(jnp.float32)).astype(jnp.bfloat16)
    counted = jnp.sum(seq_lengths).astype(jnp.float32)
    moments = (
        jnp.einsum("ti,tj->ij", act_square, grad_square, preferred_element_type=jnp.float32)
        / counted
    )
    weights = 1.0 / (moments + damping)
    act_width = gathered_act.shape[1]
    grad_width = grad_rot.shape[1]
    seq_acts = gathered_act.reshape(seq_count, seq_len, act_width)
    seq_grads = grad_rot.reshape(seq_count, seq_len, grad_width)
    seq_grad = jnp.einsum("sli,slj->sij", seq_acts, seq_grads, preferred_element_type=jnp.float32)
    scale_seq = lax.rsqrt(seq_lengths.astype(jnp.float32))
    precond = (weights[None, :, :] * seq_grad * scale_seq[:, None, None]).astype(jnp.bfloat16)
    mapped = jnp.einsum("ui,sij->suj", gathered_query, precond, preferred_element_type=jnp.float32)
    per_row = jnp.sum(mapped * query_grad_rot.astype(jnp.float32)[None, :, :], axis=2)
    per_query = jnp.sum(per_row.reshape(seq_count, QUERIES, QUERY_LEN), axis=2)
    partial_scores = per_query.T / math.sqrt(QUERY_LEN * D * FF)
    scores = lax.psum(partial_scores, ("dp", "mp"))
    return (moments, scores)


def solution(mesh):
    return jax.shard_map(
        local,
        mesh=mesh,
        in_specs=(
            P("dp", "mp"),
            P("dp", None),
            P("dp", "mp"),
            P("dp", None),
            P("mp", None),
            P("dp", None),
            P(),
        ),
        out_specs=(P("mp", "dp"), P()),
        check_vma=False,
    )
```

profile of v0, /device:TPU:0, one launch (start us, length us, event | category | flops | bytes accessed | tf_op | source)
XLA Modules:
  0.0 238.3 jit_solution(18068171213799246787)
XLA Ops:
  7.2 0.0 copy-start
  7.2 4.8 %copy.93 = bf16[16,8,8,2048]{3,2,0,1:T(8,128)(2,1)} copy(bf16[16,8,8,2048]{3,2,1,0:T(8,128)(2,1)} %bitcast.72) | data formatting | bytes 8388608 | tf_op jit(solution)/shard_map/all_to_all | solution.py:47
  12.0 0.0 copy-start.2
  12.0 0.0 copy-start.4
  12.0 0.0 copy-start.6
  12.0 5.3 %all-to-all-start = ((bf16[128,8,2048]{2,0,1:T(8,128)(2,1)}), bf16[128,8,2048]{2,0,1:T(8,128)(2,1)}, u32[]{:S(2)}, u32[]{:S(2)}) async-start(bf16[128,8,2048]{2,0,1:T(8,128)(2,1)} %bitcast.68), calls=%async_computation | async-start | bytes 8388608 | tf_op jit(solution)/shard_map/all_to_all | solution.py:47
  17.4 0.0 all-gather.3.cloned.1.call-start
  17.4 0.0 copy-done.2
  17.4 0.0 copy-done.4
  17.4 0.3 fusion.15
  17.8 0.2 copy.44
  18.0 0.0 copy-done.6
  18.0 0.1 select_reduce_fusion
  18.1 0.8 multiply_convert_fusion.4
  18.9 0.0 all-gather.3.cloned.1.call-update
  18.9 4.7 %copy.92 = bf16[16,8,8,2048]{3,2,0,1:T(8,128)(2,1)} copy(bf16[16,8,8,2048]{3,2,1,0:T(8,128)(2,1)} %bitcast.73) | data formatting | bytes 8388608 | tf_op jit(solution)/shard_map/all_to_all | solution.py:48
  23.7 51.3 %all-to-all-done = bf16[128,8,2048]{2,0,1:T(8,128)(2,1)} async-done(((bf16[128,8,2048]{2,0,1:T(8,128)(2,1)}), bf16[128,8,2048]{2,0,1:T(8,128)(2,1)}, u32[]{:S(2)}, u32[]{:S(2)}) %all-to-all-start) | async-done | bytes 4194336 | tf_op jit(solution)/shard_map/all_to_all | solution.py:47
  74.9 0.0 copy-start.3
  74.9 4.7 %all-to-all-start.1 = ((bf16[128,8,2048]{2,0,1:T(8,128)(2,1)}), bf16[128,8,2048]{2,0,1:T(8,128)(2,1)}, u32[]{:S(2)}, u32[]{:S(2)}) async-start(bf16[128,8,2048]{2,0,1:T(8,128)(2,1)} %bitcast.69), calls=%async_computation.1 | async-start | bytes 8388608 | tf_op jit(solution)/shard_map/all_to_all | solution.py:48
  79.6 0.0 all-gather.5.cloned.1.call-start
  79.7 0.0 copy-done.3
  79.7 0.3 convolution_convert_fusion
  80.0 0.9 copy.52
  80.9 0.0 all-gather.5.cloned.1.call-update
  80.9 0.6 reduce_sum.37
  82.2 3.6 %copy.67 = bf16[128,8,16,128]{3,2,1,0:T(8,128)(2,1)S(1)} copy(bf16[128,8,16,128]{3,1,2,0:T(8,128)(2,1)} %bitcast.30) | data formatting | bytes 8388608
  85.8 0.0 copy-done
  85.8 5.9 %multiply_convert_fusion.1 = (bf16[16,128,1024]{2,1,0:T(8,128)(2,1)}, bf16[16,128,1024]{2,1,0:T(8,128)(2,1)}) fusion(bf16[16,128,128]{2,1,0:T(8,128)(2,1)S(1)} %bitcast.63, bf16[1024,16,128]{2,1,0:T(8,128)(2,1)S(1)} %bitcast.65), kind=kOutput, calls=%fused_computation.4 | convolution fusion | flops 545259520 | bytes 13107200 | tf_op jit(solution)/shard_map/nbk,bkc->nbc/dot_general | solution.py:18
  91.8 7.8 %convert_element_type.86 = bf16[4,256,2048]{1,0,2:T(4,128)(2,1)} reshape(bf16[1024,16,128]{0,2,1:T(8,128)(2,1)} %bitcast.66) | data formatting | bytes 8388608 | tf_op jit(solution)/shard_map/convert_element_type | solution.py:50
  99.6 37.5 %all-to-all-done.1 = bf16[128,8,2048]{2,0,1:T(8,128)(2,1)} async-done(((bf16[128,8,2048]{2,0,1:T(8,128)(2,1)}), bf16[128,8,2048]{2,0,1:T(8,128)(2,1)}, u32[]{:S(2)}, u32[]{:S(2)}) %all-to-all-start.1) | async-done | bytes 4194336 | tf_op jit(solution)/shard_map/all_to_all | solution.py:48
  137.1 3.6 %copy.68 = bf16[128,8,16,128]{3,2,1,0:T(8,128)(2,1)S(1)} copy(bf16[128,8,16,128]{3,1,2,0:T(8,128)(2,1)} %bitcast.34) | data formatting | bytes 8388608
  140.7 5.8 %convert_convert_fusion = f32[16,128,1024]{2,1,0:T(8,128)} fusion(bf16[16,128,128]{2,1,0:T(8,128)(2,1)S(1)} %bitcast.64, bf16[1024,16,128]{2,1,0:T(8,128)(2,1)S(1)} %bitcast.67), kind=kOutput, calls=%fused_computation.12 | convolution fusion | flops 541065216 | bytes 13107200 | tf_op jit(solution)/shard_map/nbk,bkc->nbc/dot_general | solution.py:18
  146.5 0.0 all-gather.3.cloned.1.call-done
  146.5 0.0 copy-start.5
  146.5 13.9 %add_divide_fusion = (f32[1024,2048]{1,0:T(8,128)}, f32[1024,2048]{1,0:T(8,128)}) fusion(f32[]{:T(128)S(6)} %convert_element_type.84, bf16[1024,2048]{0,1:T(8,128)(2,1)} %bitcast.71, bf16[1024,1024]{1,0:T(8,128)(2,1)} %all-gather.3.cloned.1.call-done), kind=kOutput, calls=%fused_computation.3 | convolution fusion | flops 4304404480 | bytes 23068676 | tf_op jit(solution)/shard_map/ti,tj->ij/dot_general | solution.py:56
  160.4 0.0 all-gather.5.cloned.1.call-done
  160.4 0.0 copy-done.5
  160.4 0.0 copy-start.1
  160.4 30.5 %fusion = f32[4,1024]{1,0:T(4,128)S(1)} fusion(f32[1024,2048]{0,1:T(8,128)} %bitcast.70, bf16[4,256,1024]{2,1,0:T(8,128)(2,1)S(1)} %bitcast.78, f32[4]{0:T(128)S(1)} %convert_rsqrt_fusion, f32[1024,2048]{1,0:T(8,128)} %get-tuple-element.4, bf16[4,256,2048]{1,0,2:T(4,128)(2,1)} %convert_element_type.86, bf16[1024,1024]{1,0:T(8,128)(2,1)} %all-gather.5.cloned.1.call-done), kind=kOutput, calls=%fused_computation.1 | convolution fusion | flops 21516775424 | bytes 25182224 | tf_op jit(solution)/shard_map/ui,sij->suj/dot_general | solution.py:67
  191.0 0.1 reshape.108
  191.1 0.1 reduce_sum.39
  191.2 40.3 %psum.7 = f32[64,4]{0,1:T(4,128)} all-reduce(f32[64,4]{0,1:T(4,128)S(1)} %multiply_bitcast_fusion), channel_id=1, replica_groups=mesh['dp'=8,'mp'=4] {'dp','mp'}, use_global_device_ids=true, to_apply=%region_4.5 | all-reduce | flops 256 | bytes 2048 | tf_op jit(solution)/shard_map/psum | solution.py:71
  231.5 0.0 copy-done.1
  (4 shorter events, 0.0 us)
Async XLA Ops:
  7.2 78.6 %copy-start = (bf16[2048,128]{1,0:T(8,128)(2,1)S(1)}, bf16[2048,128]{1,0:T(8,128)(2,1)}, u32[]{:S(2)}) copy-start(bf16[2048,128]{1,0:T(8,128)(2,1)} %param.12) | copy-start | bytes 1572868
  12.0 5.4 %copy-start.2 = (bf16[1024,128]{1,0:T(8,128)(2,1)S(1)}, bf16[1024,128]{1,0:T(8,128)(2,1)}, u32[]{:S(2)}) copy-start(bf16[1024,128]{1,0:T(8,128)(2,1)} %param.11) | copy-start | bytes 786436
  12.0 5.4 %copy-start.4 = (bf16[128,1024]{1,0:T(8,128)(2,1)S(1)}, bf16[128,1024]{1,0:T(8,128)(2,1)}, u32[]{:S(2)}) copy-start(bf16[128,1024]{1,0:T(8,128)(2,1)} %param.7) | copy-start | bytes 786436
  12.0 6.0 %copy-start.6 = (s32[4]{0:T(128)S(1)}, s32[4]{0:T(128)}, u32[]{:S(2)}) copy-start(s32[4]{0:T(128)} %param.13) | copy-start | bytes 52
  12.0 62.9 %all-to-all-start = ((bf16[128,8,2048]{2,0,1:T(8,128)(2,1)}), bf16[128,8,2048]{2,0,1:T(8,128)(2,1)}, u32[]{:S(2)}, u32[]{:S(2)}) async-start(bf16[128,8,2048]{2,0,1:T(8,128)(2,1)} %bitcast.68), calls=%async_computation | async-start | bytes 8388608 | tf_op jit(solution)/shard_map/all_to_all | solution.py:47
  17.4 129.2 %all-gather.3.cloned.1.call-start = ((), (), s32[]{:S(2)}) async-start(), calls=%async_computation.2 | async-start | bytes 2359296 | tf_op jit(solution)/shard_map/all_gather | solution.py:43
  74.9 4.8 %copy-start.3 = (bf16[128,1024]{1,0:T(8,128)(2,1)S(1)}, bf16[128,1024]{1,0:T(8,128)(2,1)}, u32[]{:S(2)}) copy-start(bf16[128,1024]{1,0:T(8,128)(2,1)} %param.9) | copy-start | bytes 786436
  74.9 62.2 %all-to-all-start.1 = ((bf16[128,8,2048]{2,0,1:T(8,128)(2,1)}), bf16[128,8,2048]{2,0,1:T(8,128)(2,1)}, u32[]{:S(2)}, u32[]{:S(2)}) async-start(bf16[128,8,2048]{2,0,1:T(8,128)(2,1)} %bitcast.69), calls=%async_computation.1 | async-start | bytes 8388608 | tf_op jit(solution)/shard_map/all_to_all | solution.py:48
  79.6 80.8 %all-gather.5.cloned.1.call-start = ((), (), s32[]{:S(2)}) async-start(), calls=%async_computation.3 | async-start | bytes 2359296 | tf_op jit(solution)/shard_map/all_gather | solution.py:44
  146.5 13.9 %copy-start.5 = (bf16[1024,1024]{1,0:T(8,128)(2,1)S(1)}, bf16[1024,1024]{1,0:T(8,128)(2,1)}, u32[]{:S(2)}) copy-start(bf16[1024,1024]{1,0:T(8,128)(2,1)} %all-gather.3.cloned.1.call-done) | copy-start | bytes 6291460
  160.4 71.1 %copy-start.1 = (bf16[2048,128]{1,0:T(8,128)(2,1)S(1)}, bf16[2048,128]{1,0:T(8,128)(2,1)}, u32[]{:S(2)}) copy-start(bf16[2048,128]{1,0:T(8,128)(2,1)} %param.12) | copy-start | bytes 1572868
Sparse Core Ops, SparseCore 0:
  20.1 49.0 all-gather.2
  82.4 48.9 all-gather.4
where the time goes:
time: 239 us; the launch traced here: 238 us
  waiting for transfers between devices  88.8 us (37%)
  matrix products  56.8 us (24%)
  blocking collectives  40.3 us (17%)
  local copies, waits for them, and re-layouts  25.7 us (11%)
  between operations  14.8 us (6%)
  starting transfers between devices  10.1 us (4%)
    all_to_all x1, waiting for transfers between devices, local(): lax.all_to_all(grad_in, 'dp', split_axis=1, concat_axis=0, tiled=True)  51.3 us
    psum x1, blocking collectives, local(): scores = lax.psum(partial_scores, ('dp', 'mp'))  40.3 us
    all_to_all x1, waiting for transfers between devices, local(): lax.all_to_all(query_grad, 'dp', split_axis=1, concat_axis=0, tiled=True)  37.5 us
    dot_general x1, matrix products, local(): jnp.einsum('ui,sij->suj', gathered_query, precond, preferred_element_type...  30.5 us
    dot_general x1, matrix products, local(): jnp.einsum('ti,tj->ij', act_square, grad_square, preferred_element_type=j...  13.9 us
    dot_general x4, matrix products, rotate(): jnp.einsum('nbk,bkc->nbc', rows_in.reshape(count_rows, blocks, block_size...  12.4 us
    convert_element_type x1, local copies, waits for them, and re-layouts, local(): grad_rot = rotate(grad_cols, grad_basis).astype(jnp.bfloat16)  7.83 us
    unnamed x16, local copies, waits for them, and re-layouts  7.19 us
  transfers between devices with their start and end apart: 4, of which 2 were waited for; matrix products, arithmetic and copies ran while one was open for 20% of the time, Pallas kernels for 0%

commit v1 on v0

--- a/solution.py
+++ b/solution.py
@@ -68,7 +68,7 @@
     per_row = jnp.sum(mapped * query_grad_rot.astype(jnp.float32)[None, :, :], axis=2)
     per_query = jnp.sum(per_row.reshape(seq_count, QUERIES, QUERY_LEN), axis=2)
     partial_scores = per_query.T / math.sqrt(QUERY_LEN * D * FF)
-    scores = lax.psum(partial_scores, ("dp", "mp"))
+    scores = jnp.sum(lax.all_gather(partial_scores, ("dp", "mp")), axis=0)
     return (moments, scores)
 
 

time: 239 us -> 267 us (1.12)
  blocking collectives: 40.3 us -> 67.6 us
    all_gather x0 -> x1, blocking collectives: none -> 67.6 us  [local(): scores = jnp.sum(lax.all_gather(partial_scores, ('dp', 'mp')), axis=0)]
    psum x1 -> x0, blocking collectives: 40.3 us -> none  [local(): scores = lax.psum(partial_scores, ('dp', 'mp'))]
  transfers between devices with their start and end apart: 4 -> 4, of which waited for: 2 -> 2; matrix products, arithmetic and copies ran while one was open for 20% -> 18% of each run, Pallas kernels for 0% -> 0%
where the time goes in v1:
time: 267 us; the launch traced here: 266 us
  waiting for transfers between devices  88.8 us (33%)
  blocking collectives  67.6 us (25%)
  matrix products  56.8 us (21%)
  local copies, waits for them, and re-layouts  25.7 us (10%)
  between operations  14.8 us (6%)
  starting transfers between devices  10.1 us (4%)
    all_gather x1, blocking collectives, local(): scores = jnp.sum(lax.all_gather(partial_scores, ('dp', 'mp')), axis=0)  67.6 us
    all_to_all x1, waiting for transfers between devices, local(): lax.all_to_all(grad_in, 'dp', split_axis=1, concat_axis=0, tiled=True)  51.3 us
    all_to_all x1, waiting for transfers between devices, local(): lax.all_to_all(query_grad, 'dp', split_axis=1, concat_axis=0, tiled=True)  37.5 us
    dot_general x1, matrix products, local(): jnp.einsum('ui,sij->suj', gathered_query, precond, preferred_element_type...  30.5 us
    dot_general x1, matrix products, local(): jnp.einsum('ti,tj->ij', act_square, grad_square, preferred_element_type=j...  13.9 us
    dot_general x4, matrix products, rotate(): jnp.einsum('nbk,bkc->nbc', rows_in.reshape(count_rows, blocks, block_size...  12.4 us
    convert_element_type x1, local copies, waits for them, and re-layouts, local(): grad_rot = rotate(grad_cols, grad_basis).astype(jnp.bfloat16)  7.83 us
    unnamed x16, local copies, waits for them, and re-layouts  7.19 us
  transfers between devices with their start and end apart: 4, of which 2 were waited for; matrix products, arithmetic and copies ran while one was open for 18% of the time, Pallas kernels for 0%

profile of v1, /device:TPU:0, one launch (start us, length us, event | category | flops | bytes accessed | tf_op | source)
XLA Modules:
  0.0 266.3 jit_solution(2300657935739975165)
XLA Ops:
  7.2 0.0 copy-start
  7.2 4.8 %copy.108 = bf16[16,8,8,2048]{3,2,0,1:T(8,128)(2,1)} copy(bf16[16,8,8,2048]{3,2,1,0:T(8,128)(2,1)} %bitcast.74) | data formatting | bytes 8388608 | tf_op jit(solution)/shard_map/all_to_all | solution.py:47
  12.0 0.0 copy-start.2
  12.0 0.0 copy-start.4
  12.0 0.0 copy-start.6
  12.0 5.3 %all-to-all-start = ((bf16[128,8,2048]{2,0,1:T(8,128)(2,1)}), bf16[128,8,2048]{2,0,1:T(8,128)(2,1)}, u32[]{:S(2)}, u32[]{:S(2)}) async-start(bf16[128,8,2048]{2,0,1:T(8,128)(2,1)} %bitcast.70), calls=%async_computation | async-start | bytes 8388608 | tf_op jit(solution)/shard_map/all_to_all | solution.py:47
  17.4 0.0 all-gather.5.cloned.1.call-start
  17.4 0.0 copy-done.2
  17.4 0.0 copy-done.4
  17.4 0.3 fusion.15
  17.8 0.2 copy.59
  18.0 0.0 copy-done.6
  18.0 0.1 select_reduce_fusion
  18.1 0.8 multiply_convert_fusion.4
  18.9 0.0 all-gather.5.cloned.1.call-update
  18.9 4.7 %copy.107 = bf16[16,8,8,2048]{3,2,0,1:T(8,128)(2,1)} copy(bf16[16,8,8,2048]{3,2,1,0:T(8,128)(2,1)} %bitcast.75) | data formatting | bytes 8388608 | tf_op jit(solution)/shard_map/all_to_all | solution.py:48
  23.7 51.3 %all-to-all-done = bf16[128,8,2048]{2,0,1:T(8,128)(2,1)} async-done(((bf16[128,8,2048]{2,0,1:T(8,128)(2,1)}), bf16[128,8,2048]{2,0,1:T(8,128)(2,1)}, u32[]{:S(2)}, u32[]{:S(2)}) %all-to-all-start) | async-done | bytes 4194336 | tf_op jit(solution)/shard_map/all_to_all | solution.py:47
  74.9 0.0 copy-start.3
  74.9 4.7 %all-to-all-start.1 = ((bf16[128,8,2048]{2,0,1:T(8,128)(2,1)}), bf16[128,8,2048]{2,0,1:T(8,128)(2,1)}, u32[]{:S(2)}, u32[]{:S(2)}) async-start(bf16[128,8,2048]{2,0,1:T(8,128)(2,1)} %bitcast.71), calls=%async_computation.1 | async-start | bytes 8388608 | tf_op jit(solution)/shard_map/all_to_all | solution.py:48
  79.6 0.0 all-gather.7.cloned.1.call-start
  79.7 0.0 copy-done.3
  79.7 0.3 convolution_convert_fusion
  80.0 0.9 copy.67
  80.9 0.0 all-gather.7.cloned.1.call-update
  80.9 0.6 reduce_sum.46
  82.2 3.6 %copy.82 = bf16[128,8,16,128]{3,2,1,0:T(8,128)(2,1)S(1)} copy(bf16[128,8,16,128]{3,1,2,0:T(8,128)(2,1)} %bitcast.32) | data formatting | bytes 8388608
  85.8 0.0 copy-done
  85.8 5.9 %multiply_convert_fusion.1 = (bf16[16,128,1024]{2,1,0:T(8,128)(2,1)}, bf16[16,128,1024]{2,1,0:T(8,128)(2,1)}) fusion(bf16[16,128,128]{2,1,0:T(8,128)(2,1)S(1)} %bitcast.65, bf16[1024,16,128]{2,1,0:T(8,128)(2,1)S(1)} %bitcast.67), kind=kOutput, calls=%fused_computation.4 | convolution fusion | flops 545259520 | bytes 13107200 | tf_op jit(solution)/shard_map/nbk,bkc->nbc/dot_general | solution.py:18
  91.8 7.8 %convert_element_type.86 = bf16[4,256,2048]{1,0,2:T(4,128)(2,1)} reshape(bf16[1024,16,128]{0,2,1:T(8,128)(2,1)} %bitcast.68) | data formatting | bytes 8388608 | tf_op jit(solution)/shard_map/convert_element_type | solution.py:50
  99.6 37.5 %all-to-all-done.1 = bf16[128,8,2048]{2,0,1:T(8,128)(2,1)} async-done(((bf16[128,8,2048]{2,0,1:T(8,128)(2,1)}), bf16[128,8,2048]{2,0,1:T(8,128)(2,1)}, u32[]{:S(2)}, u32[]{:S(2)}) %all-to-all-start.1) | async-done | bytes 4194336 | tf_op jit(solution)/shard_map/all_to_all | solution.py:48
  137.1 3.6 %copy.83 = bf16[128,8,16,128]{3,2,1,0:T(8,128)(2,1)S(1)} copy(bf16[128,8,16,128]{3,1,2,0:T(8,128)(2,1)} %bitcast.36) | data formatting | bytes 8388608
  140.7 5.8 %convert_convert_fusion = f32[16,128,1024]{2,1,0:T(8,128)} fusion(bf16[16,128,128]{2,1,0:T(8,128)(2,1)S(1)} %bitcast.66, bf16[1024,16,128]{2,1,0:T(8,128)(2,1)S(1)} %bitcast.69), kind=kOutput, calls=%fused_computation.12 | convolution fusion | flops 541065216 | bytes 13107200 | tf_op jit(solution)/shard_map/nbk,bkc->nbc/dot_general | solution.py:18
  146.5 0.0 all-gather.5.cloned.1.call-done
  146.5 0.0 copy-start.5
  146.5 13.9 %add_divide_fusion = (f32[1024,2048]{1,0:T(8,128)}, f32[1024,2048]{1,0:T(8,128)}) fusion(f32[]{:T(128)S(6)} %convert_element_type.84, bf16[1024,2048]{0,1:T(8,128)(2,1)} %bitcast.73, bf16[1024,1024]{1,0:T(8,128)(2,1)} %all-gather.5.cloned.1.call-done), kind=kOutput, calls=%fused_computation.3 | convolution fusion | flops 4304404480 | bytes 23068676 | tf_op jit(solution)/shard_map/ti,tj->ij/dot_general | solution.py:56
  160.4 0.0 all-gather.7.cloned.1.call-done
  160.4 0.0 copy-done.5
  160.4 0.0 copy-start.1
  160.4 30.5 %fusion = f32[4,1024]{1,0:T(4,128)S(1)} fusion(f32[1024,2048]{0,1:T(8,128)} %bitcast.72, bf16[4,256,1024]{2,1,0:T(8,128)(2,1)S(1)} %bitcast.80, f32[4]{0:T(128)S(1)} %convert_rsqrt_fusion, f32[1024,2048]{1,0:T(8,128)} %get-tuple-element.4, bf16[4,256,2048]{1,0,2:T(4,128)(2,1)} %convert_element_type.86, bf16[1024,1024]{1,0:T(8,128)(2,1)} %all-gather.7.cloned.1.call-done), kind=kOutput, calls=%fused_computation.1 | convolution fusion | flops 21516775424 | bytes 25182224 | tf_op jit(solution)/shard_map/ui,sij->suj/dot_general | solution.py:67
  191.0 0.1 reshape.108
  191.1 0.1 reduce_sum.48
  191.2 67.6 %all-gather.1 = f32[32,64,4]{1,2,0:T(4,128)S(1)} all-gather(f32[1,64,4]{1,2,0:T(4,128)S(1)} %multiply_bitcast_fusion), channel_id=2, replica_groups=mesh['dp'=8,'mp'=4] {'dp','mp'}, dimensions={0}, use_global_device_ids=true | all-gather | bytes 33792 | tf_op jit(solution)/shard_map/all_gather | solution.py:71
  258.8 0.6 reduce_sum.49
  259.4 0.0 copy-done.1
  (4 shorter events, 0.0 us)
Async XLA Ops:
  7.2 78.6 %copy-start = (bf16[2048,128]{1,0:T(8,128)(2,1)S(1)}, bf16[2048,128]{1,0:T(8,128)(2,1)}, u32[]{:S(2)}) copy-start(bf16[2048,128]{1,0:T(8,128)(2,1)} %param.12) | copy-start | bytes 1572868
  12.0 5.4 %copy-start.2 = (bf16[1024,128]{1,0:T(8,128)(2,1)S(1)}, bf16[1024,128]{1,0:T(8,128)(2,1)}, u32[]{:S(2)}) copy-start(bf16[1024,128]{1,0:T(8,128)(2,1)} %param.11) | copy-start | bytes 786436
  12.0 5.4 %copy-start.4 = (bf16[128,1024]{1,0:T(8,128)(2,1)S(1)}, bf16[128,1024]{1,0:T(8,128)(2,1)}, u32[]{:S(2)}) copy-start(bf16[128,1024]{1,0:T(8,128)(2,1)} %param.7) | copy-start | bytes 786436
  12.0 6.0 %copy-start.6 = (s32[4]{0:T(128)S(1)}, s32[4]{0:T(128)}, u32[]{:S(2)}) copy-start(s32[4]{0:T(128)} %param.13) | copy-start | bytes 52
  12.0 62.9 %all-to-all-start = ((bf16[128,8,2048]{2,0,1:T(8,128)(2,1)}), bf16[128,8,2048]{2,0,1:T(8,128)(2,1)}, u32[]{:S(2)}, u32[]{:S(2)}) async-start(bf16[128,8,2048]{2,0,1:T(8,128)(2,1)} %bitcast.70), calls=%async_computation | async-start | bytes 8388608 | tf_op jit(solution)/shard_map/all_to_all | solution.py:47
  17.4 129.2 %all-gather.5.cloned.1.call-start = ((), (), s32[]{:S(2)}) async-start(), calls=%async_computation.2 | async-start | bytes 2359296 | tf_op jit(solution)/shard_map/all_gather | solution.py:43
  74.9 4.8 %copy-start.3 = (bf16[128,1024]{1,0:T(8,128)(2,1)S(1)}, bf16[128,1024]{1,0:T(8,128)(2,1)}, u32[]{:S(2)}) copy-start(bf16[128,1024]{1,0:T(8,128)(2,1)} %param.9) | copy-start | bytes 786436
  74.9 62.2 %all-to-all-start.1 = ((bf16[128,8,2048]{2,0,1:T(8,128)(2,1)}), bf16[128,8,2048]{2,0,1:T(8,128)(2,1)}, u32[]{:S(2)}, u32[]{:S(2)}) async-start(bf16[128,8,2048]{2,0,1:T(8,128)(2,1)} %bitcast.71), calls=%async_computation.1 | async-start | bytes 8388608 | tf_op jit(solution)/shard_map/all_to_all | solution.py:48
  79.6 80.8 %all-gather.7.cloned.1.call-start = ((), (), s32[]{:S(2)}) async-start(), calls=%async_computation.3 | async-start | bytes 2359296 | tf_op jit(solution)/shard_map/all_gather | solution.py:44
  146.5 13.9 %copy-start.5 = (bf16[1024,1024]{1,0:T(8,128)(2,1)S(1)}, bf16[1024,1024]{1,0:T(8,128)(2,1)}, u32[]{:S(2)}) copy-start(bf16[1024,1024]{1,0:T(8,128)(2,1)} %all-gather.5.cloned.1.call-done) | copy-start | bytes 6291460
  160.4 99.0 %copy-start.1 = (bf16[2048,128]{1,0:T(8,128)(2,1)S(1)}, bf16[2048,128]{1,0:T(8,128)(2,1)}, u32[]{:S(2)}) copy-start(bf16[2048,128]{1,0:T(8,128)(2,1)} %param.12) | copy-start | bytes 1572868
Sparse Core Ops, SparseCore 0:
  20.1 49.0 all-gather.4
  82.4 48.9 all-gather.6
